TPU v7x, 32 devices: a whole 2x2x4 slice. The times are simulated.
32 devices in a mesh: dp: 4 (over z), fsdp: 8 (over y, x, core).
Axes of the slice: x: 2, y: 2, z: 4, core: 2. Of those that a mesh axis runs over, the one named last changes fastest.
Arguments:
- images: bfloat16 [2, 64, 197, 384], P(None, ('dp', 'fsdp')), may hold values from -6 to 6
- cotangent: float32 [2, 64, 197, 384], P(None, ('dp', 'fsdp')), may hold values from -6 to 6
- image_counts: int32 [2, 32], P(None, ('dp', 'fsdp')), may hold values from 0 to 2, as said below
- ln1_gain: bfloat16 [384], P('fsdp'), may hold values from 0.5 to 1.5
- ln1_bias: bfloat16 [384], P('fsdp'), may hold values from -3 to 3
- qkv_weight: bfloat16 [384, 1152], P('fsdp'), may hold values from -1 to 1
- q_bias: bfloat16 [384], P('fsdp'), may hold values from -3 to 3
- v_bias: bfloat16 [384], P('fsdp'), may hold values from -3 to 3
- out_weight: bfloat16 [384, 384], P('fsdp'), may hold values from -1.5 to 1.5
- out_bias: bfloat16 [384], P('fsdp'), may hold values from -3 to 3
- ln2_gain: bfloat16 [384], P('fsdp'), may hold values from 0.5 to 1.5
- ln2_bias: bfloat16 [384], P('fsdp'), may hold values from -3 to 3
- fc1_weight: bfloat16 [384, 1536], P('fsdp'), may hold values from -0.3125 to 0.3125
- fc1_bias: bfloat16 [1536], P('fsdp'), may hold values from -3 to 3
- fc2_weight: bfloat16 [1536, 384], P('fsdp'), may hold values from -0.15625 to 0.15625
- fc2_bias: bfloat16 [384], P('fsdp'), may hold values from -3 to 3
Outputs:
- block_out: bfloat16 [2, 64, 197, 384], P(None, ('dp', 'fsdp'))
- image_grad: float32 [2, 64, 197, 384], P(None, ('dp', 'fsdp'))
- ln1_gain_grad: float32 [384], P('fsdp')
- ln1_bias_grad: float32 [384], P('fsdp')
- qkv_weight_grad: float32 [384, 1152], P('fsdp')
- q_bias_grad: float32 [384], P('fsdp')
- v_bias_grad: float32 [384], P('fsdp')
- out_weight_grad: float32 [384, 384], P('fsdp')
- out_bias_grad: float32 [384], P('fsdp')
- ln2_gain_grad: float32 [384], P('fsdp')
- ln2_bias_grad: float32 [384], P('fsdp')
- fc1_weight_grad: float32 [384, 1536], P('fsdp')
- fc1_bias_grad: float32 [1536], P('fsdp')
- fc2_weight_grad: float32 [1536, 384], P('fsdp')
- fc2_bias_grad: float32 [384], P('fsdp')
Inputs may be any that keep to these rules, and one draw needn't show every extreme that they name: `image_counts`: in every micro-batch some device has all 2 slots live; slots at or past a device's count are empty.
All inputs are finite; a program needn't handle non-finite values.
Results may differ from a plain program's by a relative error of at most 0.013.
The roundings to bfloat16 on the way count: a program that leaves them out, or rounds other values in their place, can miss the bound.
Values may be sent and summed in bfloat16 or wider, within the bound.
A program may use at most 128 MiB of HBM per device.

v0:
```python
import jax
import jax.numpy as jnp
from jax import lax
from jax.sharding import PartitionSpec as P

H = 6
HD = 64


def product(form, left, right):
    return jnp.einsum(form, left, right, preferred_element_type=jnp.float32)


def layer_norm(hidden):
    center = hidden - jnp.mean(hidden, axis=-1, keepdims=True)
    rstd = lax.rsqrt(jnp.mean(center * center, axis=-1, keepdims=True) + 1e-06)
    return (center * rstd, rstd)


def norm_back(grad, normed, rstd):
    return rstd * (
        grad
        - jnp.mean(grad, axis=-1, keepdims=True)
        - normed * jnp.mean(grad * normed, axis=-1, keepdims=True)
    )


def normal_cdf(value):
    return 0.5 * (1.0 + lax.erf(value * 0.7071067811865476))


def gelu_slope(value):
    return normal_cdf(value) + value * jnp.exp(-0.5 * value * value) * 0.3989422804014327


def heads(tensor):
    return tensor.reshape(tensor.shape[0], tensor.shape[1], H, HD)


def run_forward(images, weights):
    (
        gain_one,
        bias_one,
        w_qkv,
        bias_q,
        bias_v,
        w_out,
        bias_out,
        gain_two,
        bias_two,
        w_fc1,
        bias_fc1,
        w_fc2,
        bias_fc2,
    ) = weights
    width = w_qkv.shape[0]
    scale = HD ** (-0.5)
    hidden = images.astype(jnp.float32)
    normed1, rstd1 = layer_norm(hidden)
    attn_in = (normed1 * gain_one.astype(jnp.float32) + bias_one.astype(jnp.float32)).astype(
        jnp.bfloat16
    )
    mixed = product("bsd,de->bse", attn_in, w_qkv)
    query = ((mixed[..., :width] + bias_q.astype(jnp.float32)) * scale).astype(jnp.bfloat16)
    keys = mixed[..., width : 2 * width].astype(jnp.bfloat16)
    values = (mixed[..., 2 * width :] + bias_v.astype(jnp.float32)).astype(jnp.bfloat16)
    scores = product("bqhe,bkhe->bhqk", heads(query), heads(keys))
    top = jnp.max(scores, axis=-1, keepdims=True)
    expo = jnp.exp(scores - top)
    total = jnp.sum(expo, axis=-1, keepdims=True)
    probs = expo / total
    lse = top + jnp.log(total)
    attn = product("bhqk,bkhe->bqhe", probs.astype(jnp.bfloat16), heads(values))
    attn = attn.reshape(hidden.shape).astype(jnp.bfloat16)
    resid = hidden + product("bsd,de->bse", attn, w_out) + bias_out.astype(jnp.float32)
    normed2, rstd2 = layer_norm(resid)
    mlp_in = (normed2 * gain_two.astype(jnp.float32) + bias_two.astype(jnp.float32)).astype(
        jnp.bfloat16
    )
    pre = product("bsd,df->bsf", mlp_in, w_fc1) + bias_fc1.astype(jnp.float32)
    act = (pre * normal_cdf(pre)).astype(jnp.bfloat16)
    result = resid + product("bsf,fd->bsd", act, w_fc2) + bias_fc2.astype(jnp.float32)
    saved = (
        normed1,
        rstd1,
        attn_in,
        query,
        keys,
        values,
        lse,
        attn,
        normed2,
        rstd2,
        mlp_in,
        pre,
        act,
    )
    return (result, saved)


def run_backward(cot, saved, weights):
    (
        gain_one,
        bias_one,
        w_qkv,
        bias_q,
        bias_v,
        w_out,
        bias_out,
        gain_two,
        bias_two,
        w_fc1,
        bias_fc1,
        w_fc2,
        bias_fc2,
    ) = weights
    normed1, rstd1, attn_in, query, keys, values, lse, attn, normed2, rstd2, mlp_in, pre, act = (
        saved
    )
    scale = HD ** (-0.5)
    rows = (0, 1)
    grad_b = cot.astype(jnp.bfloat16)
    grad_fc2 = product("bsf,bsd->fd", act, grad_b)
    grad_bias_fc2 = jnp.sum(cot, axis=rows)
    d_pre = product("bsd,fd->bsf", grad_b, w_fc2) * gelu_slope(pre)
    d_pre_b = d_pre.astype(jnp.bfloat16)
    grad_fc1 = product("bsd,bsf->df", mlp_in, d_pre_b)
    grad_bias_fc1 = jnp.sum(d_pre, axis=rows)
    d_mlp = product("bsf,df->bsd", d_pre_b, w_fc1)
    grad_gain_two = jnp.sum(d_mlp * normed2, axis=rows)
    grad_bias_two = jnp.sum(d_mlp, axis=rows)
    d_resid = cot + norm_back(d_mlp * gain_two.astype(jnp.float32), normed2, rstd2)
    d_proj = d_resid.astype(jnp.bfloat16)
    grad_out = product("bsd,bse->de", attn, d_proj)
    grad_bias_out = jnp.sum(d_resid, axis=rows)
    d_attn = product("bse,de->bsd", d_proj, w_out).astype(jnp.bfloat16)
    scores = product("bqhe,bkhe->bhqk", heads(query), heads(keys))
    probs = jnp.exp(scores - lse)
    d_values = product("bhqk,bqhe->bkhe", probs.astype(jnp.bfloat16), heads(d_attn))
    d_probs = product("bqhe,bkhe->bhqk", heads(d_attn), heads(values))
    delta = jnp.sum(probs * d_probs, axis=-1, keepdims=True)
    d_scores = (probs * (d_probs - delta)).astype(jnp.bfloat16)
    d_query = product("bhqk,bkhe->bqhe", d_scores, heads(keys)) * scale
    d_keys = product("bhqk,bqhe->bkhe", d_scores, heads(query))
    shape = d_resid.shape
    d_query = d_query.reshape(shape)
    d_keys = d_keys.reshape(shape)
    d_values = d_values.reshape(shape)
    d_mixed = jnp.concatenate([d_query, d_keys, d_values], axis=-1).astype(jnp.bfloat16)
    grad_qkv = product("bsd,bse->de", attn_in, d_mixed)
    grad_bias_q = jnp.sum(d_query, axis=rows)
    grad_bias_v = jnp.sum(d_values, axis=rows)
    d_in = product("bse,de->bsd", d_mixed, w_qkv)
    grad_gain_one = jnp.sum(d_in * normed1, axis=rows)
    grad_bias_one = jnp.sum(d_in, axis=rows)
    d_images = d_resid + norm_back(d_in * gain_one.astype(jnp.float32), normed1, rstd1)
    grads = (
        grad_gain_one,
        grad_bias_one,
        grad_qkv,
        grad_bias_q,
        grad_bias_v,
        grad_out,
        grad_bias_out,
        grad_gain_two,
        grad_bias_two,
        grad_fc1,
        grad_bias_fc1,
        grad_fc2,
        grad_bias_fc2,
    )
    return (d_images, grads)


def shards(
    images,
    cotangent,
    image_counts,
    ln1_gain,
    ln1_bias,
    qkv_weight,
    q_bias,
    v_bias,
    out_weight,
    out_bias,
    ln2_gain,
    ln2_bias,
    fc1_weight,
    fc1_bias,
    fc2_weight,
    fc2_bias,
):
    micro_count = images.shape[0]
    slot_count = images.shape[1]
    results = []
    d_results = []
    totals = None
    for micro_index in range(micro_count):
        alive = (jnp.arange(slot_count) < image_counts[micro_index, 0]).astype(jnp.float32)[
            :, None, None
        ]
        weights = (
            lax.all_gather(ln1_gain, "fsdp", axis=0, tiled=True),
            lax.all_gather(ln1_bias, "fsdp", axis=0, tiled=True),
            lax.all_gather(qkv_weight, "fsdp", axis=0, tiled=True),
            lax.all_gather(q_bias, "fsdp", axis=0, tiled=True),
            lax.all_gather(v_bias, "fsdp", axis=0, tiled=True),
            lax.all_gather(out_weight, "fsdp", axis=0, tiled=True),
            lax.all_gather(out_bias, "fsdp", axis=0, tiled=True),
            lax.all_gather(ln2_gain, "fsdp", axis=0, tiled=True),
            lax.all_gather(ln2_bias, "fsdp", axis=0, tiled=True),
            lax.all_gather(fc1_weight, "fsdp", axis=0, tiled=True),
            lax.all_gather(fc1_bias, "fsdp", axis=0, tiled=True),
            lax.all_gather(fc2_weight, "fsdp", axis=0, tiled=True),
            lax.all_gather(fc2_bias, "fsdp", axis=0, tiled=True),
        )
        result, saved = run_forward(images[micro_index], weights)
        results.append((result * alive).astype(jnp.bfloat16))
        back_weights = (
            lax.all_gather(ln1_gain, "fsdp", axis=0, tiled=True),
            lax.all_gather(ln1_bias, "fsdp", axis=0, tiled=True),
            lax.all_gather(qkv_weight, "fsdp", axis=0, tiled=True),
            lax.all_gather(q_bias, "fsdp", axis=0, tiled=True),
            lax.all_gather(v_bias, "fsdp", axis=0, tiled=True),
            lax.all_gather(out_weight, "fsdp", axis=0, tiled=True),
            lax.all_gather(out_bias, "fsdp", axis=0, tiled=True),
            lax.all_gather(ln2_gain, "fsdp", axis=0, tiled=True),
            lax.all_gather(ln2_bias, "fsdp", axis=0, tiled=True),
            lax.all_gather(fc1_weight, "fsdp", axis=0, tiled=True),
            lax.all_gather(fc1_bias, "fsdp", axis=0, tiled=True),
            lax.all_gather(fc2_weight, "fsdp", axis=0, tiled=True),
            lax.all_gather(fc2_bias, "fsdp", axis=0, tiled=True),
        )
        d_images, grads = run_backward(cotangent[micro_index] * alive, saved, back_weights)
        d_results.append(d_images)
        if totals is None:
            totals = grads
        else:
            totals = jax.tree.map(lambda acc, new: acc + new, totals, grads)
    totals = (
        lax.psum_scatter(totals[0], "fsdp", scatter_dimension=0, tiled=True),
        lax.psum_scatter(totals[1], "fsdp", scatter_dimension=0, tiled=True),
        lax.psum_scatter(totals[2], "fsdp", scatter_dimension=0, tiled=True),
        lax.psum_scatter(totals[3], "fsdp", scatter_dimension=0, tiled=True),
        lax.psum_scatter(totals[4], "fsdp", scatter_dimension=0, tiled=True),
        lax.psum_scatter(totals[5], "fsdp", scatter_dimension=0, tiled=True),
        lax.psum_scatter(totals[6], "fsdp", scatter_dimension=0, tiled=True),
        lax.psum_scatter(totals[7], "fsdp", scatter_dimension=0, tiled=True),
        lax.psum_scatter(totals[8], "fsdp", scatter_dimension=0, tiled=True),
        lax.psum_scatter(totals[9], "fsdp", scatter_dimension=0, tiled=True),
        lax.psum_scatter(totals[10], "fsdp", scatter_dimension=0, tiled=True),
        lax.psum_scatter(totals[11], "fsdp", scatter_dimension=0, tiled=True),
        lax.psum_scatter(totals[12], "fsdp", scatter_dimension=0, tiled=True),
    )
    totals = (
        lax.psum(totals[0].astype(jnp.bfloat16), "dp").astype(jnp.float32),
        lax.psum(totals[1].astype(jnp.bfloat16), "dp").astype(jnp.float32),
        lax.psum(totals[2].astype(jnp.bfloat16), "dp").astype(jnp.float32),
        lax.psum(totals[3].astype(jnp.bfloat16), "dp").astype(jnp.float32),
        lax.psum(totals[4].astype(jnp.bfloat16), "dp").astype(jnp.float32),
        lax.psum(totals[5].astype(jnp.bfloat16), "dp").astype(jnp.float32),
        lax.psum(totals[6].astype(jnp.bfloat16), "dp").astype(jnp.float32),
        lax.psum(totals[7].astype(jnp.bfloat16), "dp").astype(jnp.float32),
        lax.psum(totals[8].astype(jnp.bfloat16), "dp").astype(jnp.float32),
        lax.psum(totals[9].astype(jnp.bfloat16), "dp").astype(jnp.float32),
        lax.psum(totals[10].astype(jnp.bfloat16), "dp").astype(jnp.float32),
        lax.psum(totals[11].astype(jnp.bfloat16), "dp").astype(jnp.float32),
        lax.psum(totals[12].astype(jnp.bfloat16), "dp").astype(jnp.float32),
    )
    block_out = jnp.stack(results, axis=0)
    image_grad = jnp.stack(d_results, axis=0)
    return (
        block_out,
        image_grad,
        totals[0],
        totals[1],
        totals[2],
        totals[3],
        totals[4],
        totals[5],
        totals[6],
        totals[7],
        totals[8],
        totals[9],
        totals[10],
        totals[11],
        totals[12],
    )


def solution(mesh):
    placed = (
        P(None, ("dp", "fsdp"), None, None),
        P(None, ("dp", "fsdp"), None, None),
        P(None, ("dp", "fsdp")),
        P("fsdp"),
        P("fsdp"),
        P("fsdp", None),
        P("fsdp"),
        P("fsdp"),
        P("fsdp", None),
        P("fsdp"),
        P("fsdp"),
        P("fsdp"),
        P("fsdp", None),
        P("fsdp"),
        P("fsdp", None),
        P("fsdp"),
    )
    return jax.shard_map(
        shards,
        mesh=mesh,
        in_specs=placed,
        out_specs=(
            P(None, ("dp", "fsdp"), None, None),
            P(None, ("dp", "fsdp"), None, None),
            P("fsdp"),
            P("fsdp"),
            P("fsdp", None),
            P("fsdp"),
            P("fsdp"),
            P("fsdp", None),
            P("fsdp"),
            P("fsdp"),
            P("fsdp"),
            P("fsdp", None),
            P("fsdp"),
            P("fsdp", None),
            P("fsdp"),
        ),
        check_vma=False,
    )
```

profile of v0, /device:TPU:0, one launch (start us, length us, event | category | flops | bytes accessed | tf_op | source)
XLA Modules:
  0.0 349.3 jit_solution(17786109639577398773)
XLA Ops:
  19.0 25.7 %all-reduce.19 = (bf16[384]{0:T(512)(128)(2,1)S(1)}, bf16[384]{0:T(512)(128)(2,1)S(1)}, bf16[384]{0:T(512)(128)(2,1)S(1)}, bf16[384]{0:T(512)(128)(2,1)S(1)}, bf...) all-reduce(bf16[384]{0:T(512)(128)(2,1)S(1)} %dynamic-update-slice., ...), channel_id=1, replica_groups=mesh['dp'=4,'fsdp'=8] {'fsdp'}, use_global_device_ids=true, to_apply=%add.1 | all-reduce | flops 4608 | bytes 18432
  44.6 11.2 %all_gather.28 = bf16[384,1152]{1,0:T(8,128)(2,1)S(1)} all-gather(bf16[48,1152]{1,0:T(8,128)(2,1)} %param.21), channel_id=1, replica_groups=mesh['dp'=4,'fsdp'=8] {'fsdp'}, dimensions={0}, use_global_device_ids=true | all-gather | bytes 995328 | tf_op jit(solution)/shard_map/all_gather | solution.py:205
  61.0 8.8 %all_gather.31 = bf16[384,384]{1,0:T(8,128)(2,1)S(1)} all-gather(bf16[48,384]{1,0:T(8,128)(2,1)S(1)} %copy-done.60), channel_id=1, replica_groups=mesh['dp'=4,'fsdp'=8] {'fsdp'}, dimensions={0}, use_global_device_ids=true | all-gather | bytes 331776 | tf_op jit(solution)/shard_map/all_gather | solution.py:208
  83.3 4.5 %multiply_convert_fusion.3 = (bf16[2,197,1536]{2,1,0:T(8,128)(2,1)}, f32[2,197,1536]{2,1,0:T(8,128)}) fusion(f32[1536]{0:T(1024)S(1)} %convert_element_type.261, bf16[384,1536]{1,0:T(8,128)(2,1)} %all-gather.3.cloned.1.call-done, f32[2,197,384]{2,1,0:T(8,128)} %copy-done.28, f32[384]{0:T(512)S(1)} %convert_element_type.259, ...), kind=kOutput, calls=%fused_computation.33 | convolution fusion | flops 469168896 | bytes 5428304 | tf_op jit(solution)/shard_map/bsd,df->bsf/dot_general | solution.py:11
  87.8 4.4 %fusion.136 = (f32[1536]{0:T(1024)}, bf16[2,197,1536]{2,1,0:T(8,128)(2,1)S(1)}) fusion(f32[2,197,1536]{2,1,0:T(8,128)} %get-tuple-element.157, bf16[1536,384]{1,0:T(8,128)(2,1)} %all-gather.5.cloned.1.call-done, f32[1,2,197,384]{3,1,2,0:T(2,128)} %get-tuple-element.115, f32[2]{0:T(128)S(1)} %compare_convert_fusion.1), kind=kOutput, calls=%fused_computation.229 | convolution fusion | flops 471739392 | bytes 5422088 | tf_op jit(solution)/shard_map/bsd,fd->bsf/dot_general | solution.py:11
  93.7 2.3 multiply_convert_fusion.2
  96.0 2.3 fusion.137
  98.3 2.4 fusion.123
  104.7 3.3 fusion.125
  115.1 2.3 fusion.126
  124.2 1.9 convolution_bitcast_fusion.5
  126.2 2.1 fusion
  128.4 2.3 convolution_bitcast_fusion.2
  130.8 2.4 fusion.1
  134.3 2.4 convolution_bitcast_fusion
  136.8 2.5 fusion.2
  141.3 2.6 fusion.31
  152.7 15.1 %reduce-scatter.5.cloned.1.call-done = f32[48,1152]{1,0:T(8,128)} async-done(((f32[384,1152]{1,0:T(8,128)}), f32[48,1152]{1,0:T(8,128)}) %reduce-scatter.5.cloned.1.call-update) | async-done | bytes 221200 | tf_op jit(solution)/shard_map/reduce_scatter | solution.py:243
  169.4 44.0 %reduce-scatter.9.cloned.1.call-done = f32[48,1536]{1,0:T(8,128)} async-done(((f32[384,1536]{1,0:T(8,128)}), f32[48,1536]{1,0:T(8,128)}) %reduce-scatter.9.cloned.1.call-update) | async-done | bytes 294928 | tf_op jit(solution)/shard_map/reduce_scatter | solution.py:250
  215.1 43.9 %reduce-scatter.11.cloned.1.call-done = f32[192,384]{1,0:T(8,128)} async-done(((f32[1536,384]{1,0:T(8,128)}), f32[192,384]{1,0:T(8,128)}) %reduce-scatter.11.cloned.1.call-update) | async-done | bytes 294928 | tf_op jit(solution)/shard_map/reduce_scatter | solution.py:252
  263.1 22.9 %all-reduce.18 = (bf16[384]{0:T(512)(128)(2,1)S(1)}, bf16[384]{0:T(512)(128)(2,1)S(1)}, bf16[384]{0:T(512)(128)(2,1)S(1)}, bf16[384]{0:T(512)(128)(2,1)S(1)}, bf...) all-reduce(f32[384]{0:T(512)S(1)} %add.320, ...), channel_id=2, replica_groups=mesh['dp'=4,'fsdp'=8] {'fsdp'}, use_global_device_ids=true, to_apply=%region_24.0.clone | all-reduce | flops 4608 | bytes 27648
  286.7 9.7 %reduce-scatter.7.cloned.1.call-done = f32[48,384]{1,0:T(8,128)} async-done(((f32[384,384]{1,0:T(8,128)}), f32[48,384]{1,0:T(8,128)}) %reduce-scatter.7.cloned.1.call-update) | async-done | bytes 73744 | tf_op jit(solution)/shard_map/reduce_scatter | solution.py:246
  297.3 19.8 %all-reduce.20 = (bf16[48]{0:T(256)(128)(2,1)S(1)}, bf16[48]{0:T(256)(128)(2,1)S(1)}, bf16[48]{0:T(256)(128)(2,1)S(1)}, bf16[48]{0:T(256)(128)(2,1)S(1)}, bf16[4...) all-reduce(bf16[48]{0:T(256)(128)(2,1)S(1)} %dynamic-slice.44, ...), channel_id=1, replica_groups=mesh['dp'=4,'fsdp'=8] {'dp'}, use_global_device_ids=true, to_apply=%region_25.0 | all-reduce | flops 19008 | bytes 76032 | tf_op jit(solution)/shard_map/psum | solution.py:256
  322.4 15.2 %all-reduce.24.cloned.1.call-done = (bf16[48,1152]{1,0:T(8,128)(2,1)}, bf16[48,1536]{1,0:T(8,128)(2,1)}, bf16[192,384]{1,0:T(8,128)(2,1)}) async-done(((bf16[48,1152]{1,0:T(8,128)(2,1)}, bf16[48,1536]{1,0:T(8,128)(2,1)}, bf16[192,384]{1,0:T(8,128)(2,1)}), (bf16[48,1152]{1,0:T(8,128)(2,1)}, bf16[48,1536]{1,0:T(8,128)(2,1)}, bf16[192,384]{1,0:T(8,128)(2,1)})) %all-reduce.24.cloned.1.call-update) | async-done | bytes 405520 | tf_op jit(solution)/shard_map/psum | solution.py:258
  (323 shorter events, 77.4 us)
Async XLA Ops:
  7.2 76.2 %all-gather.3.cloned.1.call-start = ((), (), s32[]{:S(2)}) async-start(), calls=%async_computation.4 | async-start | bytes 1327104 | tf_op jit(solution)/shard_map/all_gather | solution.py:212
  7.9 79.9 %all-gather.5.cloned.1.call-start = ((), (), s32[]{:S(2)}) async-start(), calls=%async_computation.5 | async-start | bytes 1327104 | tf_op jit(solution)/shard_map/all_gather | solution.py:214
  8.7 159.2 %reduce-scatter.5.cloned.1.call-start = ((), (), s32[]{:S(2)}) async-start(), calls=%async_computation.6 | async-start | bytes 1990656 | tf_op jit(solution)/shard_map/reduce_scatter | solution.py:243
  55.8 3.4 copy-start.2
  57.7 22.3 %copy-start.4 = (bf16[1,2,197,384]{3,1,2,0:T(2,128)(2,1)}, bf16[1,2,197,384]{3,1,2,0:T(2,128)(2,1)S(1)}, u32[]{:S(2)}) copy-start(bf16[1,2,197,384]{3,1,2,0:T(2,128)(2,1)S(1)} %get-tuple-element.127) | copy-start | bytes 907780
  60.6 10.2 %copy-start.34 = (bf16[2,197,384]{1,2,0:T(8,128)(2,1)}, bf16[2,197,384]{1,2,0:T(8,128)(2,1)S(1)}, u32[]{:S(2)}) copy-start(bf16[2,197,384]{1,2,0:T(8,128)(2,1)S(1)} %copy.110) | copy-start | bytes 907780
  60.8 10.0 %copy-start.20 = (bf16[2,197,384]{1,2,0:T(8,128)(2,1)}, bf16[2,197,384]{1,2,0:T(8,128)(2,1)S(1)}, u32[]{:S(2)}) copy-start(bf16[2,197,384]{1,2,0:T(8,128)(2,1)S(1)} %copy.111) | copy-start | bytes 907780
  61.0 9.8 %copy-start.17 = (bf16[2,197,384]{1,2,0:T(8,128)(2,1)}, bf16[2,197,384]{1,2,0:T(8,128)(2,1)S(1)}, u32[]{:S(2)}) copy-start(bf16[2,197,384]{1,2,0:T(8,128)(2,1)S(1)} %copy.112) | copy-start | bytes 907780
  71.8 5.3 %copy-start.47 = (bf16[2,6,64,197]{3,2,1,0:T(8,128)(2,1)}, bf16[2,6,64,197]{3,2,1,0:T(8,128)(2,1)S(1)}, u32[]{:S(2)}) copy-start(bf16[2,6,64,197]{3,2,1,0:T(8,128)(2,1)S(1)} %convolution_convert_fusion.2) | copy-start | bytes 907780
  74.3 26.4 %copy-start.67 = (f32[2]{0:T(128)}, f32[2]{0:T(128)S(1)}, u32[]{:S(2)}) copy-start(f32[2]{0:T(128)S(1)} %compare_convert_fusion) | copy-start | bytes 28
  81.4 16.9 %copy-start.77 = (f32[2]{0:T(128)}, f32[2]{0:T(128)S(1)}, u32[]{:S(2)}) copy-start(f32[2]{0:T(128)S(1)} %compare_convert_fusion.1) | copy-start | bytes 28
  82.0 16.3 %copy-start.61 = (f32[2,197]{1,0:T(2,128)}, f32[2,197]{1,0:T(2,128)S(1)}, u32[]{:S(2)}) copy-start(f32[2,197]{1,0:T(2,128)S(1)} %add_rsqrt_fusion.2) | copy-start | bytes 4732
  83.3 12.6 %copy-start.11 = (f32[1,2,197,384]{3,1,2,0:T(2,128)}, f32[1,2,197,384]{3,1,2,0:T(2,128)S(1)}, u32[]{:S(2)}) copy-start(f32[1,2,197,384]{3,1,2,0:T(2,128)S(1)} %get-tuple-element.116) | copy-start | bytes 1815556
  87.8 4.4 %copy-start.29 = (f32[2,197,384]{2,1,0:T(8,128)S(1)}, f32[2,197,384]{2,1,0:T(8,128)}, u32[]{:S(2)}) copy-start(f32[2,197,384]{2,1,0:T(8,128)} %copy-done.28) | copy-start | bytes 1815556
  87.8 4.4 %copy-start.81 = (bf16[384,1536]{1,0:T(8,128)(2,1)S(1)}, bf16[384,1536]{1,0:T(8,128)(2,1)}, u32[]{:S(2)}) copy-start(bf16[384,1536]{1,0:T(8,128)(2,1)} %all-gather.3.cloned.1.call-done) | copy-start | bytes 3538948
  92.2 3.8 %copy-start.41 = (bf16[2,197,1536]{2,1,0:T(8,128)(2,1)}, bf16[2,197,1536]{2,1,0:T(8,128)(2,1)S(1)}, u32[]{:S(2)}) copy-start(bf16[2,197,1536]{2,1,0:T(8,128)(2,1)S(1)} %get-tuple-element.164) | copy-start | bytes 3631108
  124.2 4.1 %copy-start.58 = (bf16[2,197,384]{2,1,0:T(8,128)(2,1)}, bf16[2,197,384]{2,1,0:T(8,128)(2,1)S(1)}, u32[]{:S(2)}) copy-start(bf16[2,197,384]{2,1,0:T(8,128)(2,1)S(1)} %copy.120) | copy-start | bytes 907780
  128.3 85.1 %reduce-scatter.9.cloned.1.call-start = ((), (), s32[]{:S(2)}) async-start(), calls=%async_computation.8 | async-start | bytes 2654208 | tf_op jit(solution)/shard_map/reduce_scatter | solution.py:250
  133.2 3.5 %copy-start.27 = (f32[1,2,197,384]{3,1,2,0:T(2,128)S(1)}, f32[1,2,197,384]{3,1,2,0:T(2,128)}, u32[]{:S(2)}) copy-start(f32[1,2,197,384]{3,1,2,0:T(2,128)} %get-tuple-element.115) | copy-start | bytes 1815556
  133.2 3.5 %copy-start.78 = (f32[2]{0:T(128)S(1)}, f32[2]{0:T(128)}, u32[]{:S(2)}) copy-start(f32[2]{0:T(128)} %copy-done.77) | copy-start | bytes 28
  133.2 125.8 %reduce-scatter.11.cloned.1.call-start = ((), (), s32[]{:S(2)}) async-start(), calls=%async_computation.9 | async-start | bytes 2654208 | tf_op jit(solution)/shard_map/reduce_scatter | solution.py:252
  139.3 4.6 %copy-start.31 = (f32[2,197,384]{2,1,0:T(8,128)S(1)}, f32[2,197,384]{2,1,0:T(8,128)}, u32[]{:S(2)}) copy-start(f32[2,197,384]{2,1,0:T(8,128)} %copy-done.28) | copy-start | bytes 1815556
  139.3 157.1 %reduce-scatter.7.cloned.1.call-start = ((), (), s32[]{:S(2)}) async-start(), calls=%async_computation.7 | async-start | bytes 663552 | tf_op jit(solution)/shard_map/reduce_scatter | solution.py:246
  150.9 186.7 %all-reduce.24.cloned.1.call-start = ((), (), s32[]{:S(2)}) async-start(), calls=%async_computation.10 | async-start | bytes 811008 | tf_op jit(solution)/shard_map/psum | solution.py:258
  (65 other events, 133.8 us)
Sparse Core Ops, SparseCore 0:
  9.9 26.7 all-gather.2
  38.6 25.0 all-gather.4
  128.4 39.3 reduce-scatter.4
  171.1 42.3 reduce-scatter.8
  216.6 42.3 reduce-scatter.10
  262.0 34.3 reduce-scatter.6
  300.1 37.4 all-reduce.23
where the time goes:
time: 350 us; the launch traced here: 349 us
  waiting for transfers between devices  129 us (37%)
  blocking collectives  88.3 us (25%)
  matrix products  58.3 us (17%)
  local copies, waits for them, and re-layouts  30.9 us (9%)
  other arithmetic  23.8 us (7%)
  between operations  18 us (5%)
    dot_general x36, matrix products, product(): return jnp.einsum(form, left, right, preferred_element_type=jnp.float32)  58.3 us
    unnamed x2, blocking collectives  48.6 us
    reduce_scatter x1, waiting for transfers between devices, shards(): lax.psum_scatter(totals[9], 'fsdp', scatter_dimension=0, tiled=True)  44 us
    reduce_scatter x1, waiting for transfers between devices, shards(): lax.psum_scatter(totals[11], 'fsdp', scatter_dimension=0, tiled=True)  43.9 us
    psum x1, blocking collectives, shards(): lax.psum(totals[0].astype(jnp.bfloat16), 'dp').astype(jnp.float32)  19.8 us
    unnamed x194, local copies, waits for them, and re-layouts  16.6 us
    psum x1, waiting for transfers between devices, shards(): lax.psum(totals[2].astype(jnp.bfloat16), 'dp').astype(jnp.float32)  15.2 us
    reduce_scatter x1, waiting for transfers between devices, shards(): lax.psum_scatter(totals[2], 'fsdp', scatter_dimension=0, tiled=True)  15.1 us
  transfers between devices with their start and end apart: 7, of which 5 were waited for; matrix products, arithmetic and copies ran while one was open for 19% of the time, Pallas kernels for 0%

commit v1 on v0

v1 whole, which is shorter than its diff:
```python
import functools

import jax
import jax.numpy as jnp
from jax import lax
from jax.experimental import pallas as pl
from jax.experimental.pallas import tpu as pltpu
from jax.sharding import PartitionSpec as P

H = 6
HD = 64
LANE = 128
BLOCKS = 8
SMALL = 16


def dot(left, right, left_dim, right_dim):
    return lax.dot_general(
        left,
        right,
        (((left_dim,), (right_dim,)), ((), ())),
        preferred_element_type=jnp.float32,
    )


def layer_norm(hidden):
    center = hidden - jnp.mean(hidden, axis=-1, keepdims=True)
    rstd = lax.rsqrt(jnp.mean(center * center, axis=-1, keepdims=True) + 1e-06)
    return (center * rstd, rstd)


def norm_back(grad, normed, rstd):
    return rstd * (
        grad
        - jnp.mean(grad, axis=-1, keepdims=True)
        - normed * jnp.mean(grad * normed, axis=-1, keepdims=True)
    )


def block_kernel(
    last, tokens, alive_ref, img_ref, cot_ref, w_ref, out_ref, dimg_ref, g_ref,
    hid, cot, acc, sacc, probs_s, q_s, k_s, v_s, attn_s,
):
    step = pl.program_id(0)
    width = hid.shape[1]
    rows = hid.shape[0]
    part = width // BLOCKS
    ff_parts = (w_ref.shape[1] - SMALL - 4 * part) // (2 * part)
    bf16 = jnp.bfloat16
    f32 = jnp.float32

    @pl.when(step == 0)
    def _():
        hid[...] = jnp.zeros_like(hid)
        cot[...] = jnp.zeros_like(cot)
        acc[...] = jnp.zeros_like(acc)
        sacc[...] = jnp.zeros_like(sacc)

    alive = alive_ref[step]
    hid[0:tokens, :] = img_ref[0].astype(f32)
    cot[0:tokens, :] = cot_ref[0] * alive

    small = jnp.sum(w_ref[:, w_ref.shape[1] - SMALL :, :].astype(f32), axis=0)

    def vec(index):
        return small[index : index + 1, :]

    def weight(index):
        return w_ref[:, index * part : (index + 1) * part, :].reshape(width, width)

    def add(index, value):
        acc[:, index * part : (index + 1) * part, :] += value.reshape(BLOCKS, part, width)

    def fc2(index):
        start = (4 + ff_parts) * part
        chunk = BLOCKS // ff_parts
        return w_ref[index * chunk : (index + 1) * chunk, start : start + ff_parts * part, :].reshape(width, width)

    def add_fc2(index, value):
        start = (4 + ff_parts) * part
        chunk = BLOCKS // ff_parts
        acc[index * chunk : (index + 1) * chunk, start : start + ff_parts * part, :] += value.reshape(
            chunk, ff_parts * part, width
        )

    def add_small(index, value):
        sacc[index : index + 1, :] += jnp.sum(value, axis=0, keepdims=True)

    scale = HD ** (-0.5)
    normed1, rstd1 = layer_norm(hid[...])
    attn_in = (normed1 * vec(0) + vec(1)).astype(bf16)
    q_s[...] = ((dot(attn_in, weight(0), 1, 0) + vec(2)) * scale).astype(bf16)
    k_s[...] = dot(attn_in, weight(1), 1, 0).astype(bf16)
    v_s[...] = (dot(attn_in, weight(2), 1, 0) + vec(3)).astype(bf16)

    low = lax.broadcasted_iota(jnp.int32, (1, LANE), 1) < HD
    masks = (low.astype(f32).astype(bf16), (1.0 - low.astype(f32)).astype(bf16))
    keymask = lax.broadcasted_iota(jnp.int32, (rows, rows), 1) < tokens
    for pair in range(H // 2):
        cols = slice(pair * LANE, (pair + 1) * LANE)
        q, k, v = q_s[:, cols], k_s[:, cols], v_s[:, cols]
        halves = []
        for side in range(2):
            scores = jnp.where(keymask, dot(q * masks[side], k, 1, 1), -1e30)
            expo = jnp.exp(scores - jnp.max(scores, axis=-1, keepdims=True))
            probs = expo * (1.0 / jnp.sum(expo, axis=-1, keepdims=True))
            probs_s[2 * pair + side] = probs
            halves.append(dot(probs.astype(bf16), v, 1, 0))
        attn_s[:, cols] = jnp.where(low, halves[0], halves[1]).astype(bf16)

    attn = attn_s[...]
    resid = hid[...] + dot(attn, weight(3), 1, 0) + vec(4)
    normed2, rstd2 = layer_norm(resid)
    mlp_in = (normed2 * vec(5) + vec(6)).astype(bf16)
    grad_top = cot[...]
    dy = grad_top.astype(bf16)
    add_small(7, grad_top)
    result = resid + vec(7)
    d_mlp = jnp.zeros_like(resid)
    for index in range(ff_parts):
        w_one = weight(4 + index)
        w_two = fc2(index)
        pre = dot(mlp_in, w_one, 1, 0) + vec(8 + index)
        cdf = 0.5 * (1.0 + lax.erf(pre * 0.7071067811865476))
        slope = cdf + pre * jnp.exp(-0.5 * pre * pre) * 0.3989422804014327
        act = (pre * cdf).astype(bf16)
        result = result + dot(act, w_two, 1, 0)
        add_fc2(index, dot(act, dy, 0, 0))
        d_pre = dot(dy, w_two, 1, 1) * slope
        d_pre_b = d_pre.astype(bf16)
        add_small(8 + index, d_pre)
        add(4 + index, dot(mlp_in, d_pre_b, 0, 0))
        d_mlp = d_mlp + dot(d_pre_b, w_one, 1, 1)
    out_ref[0] = (result * alive)[0:tokens, :].astype(bf16)

    add_small(5, d_mlp * normed2)
    add_small(6, d_mlp)
    d_resid = grad_top + norm_back(d_mlp * vec(5), normed2, rstd2)
    d_proj = d_resid.astype(bf16)
    add(3, dot(attn, d_proj, 0, 0))
    add_small(4, d_resid)
    attn_s[...] = dot(d_proj, weight(3), 1, 1).astype(bf16)
    for pair in range(H // 2):
        cols = slice(pair * LANE, (pair + 1) * LANE)
        q, k, v, d_attn = q_s[:, cols], k_s[:, cols], v_s[:, cols], attn_s[:, cols]
        d_q, d_k, d_v = [], [], []
        for side in range(2):
            probs = probs_s[2 * pair + side]
            d_v.append(dot(probs.astype(bf16), d_attn, 0, 0))
            d_probs = dot(d_attn * masks[side], v, 1, 1)
            delta = jnp.sum(probs * d_probs, axis=-1, keepdims=True)
            d_scores = (probs * (d_probs - delta)).astype(bf16)
            d_q.append(dot(d_scores, k, 1, 0))
            d_k.append(dot(d_scores, q, 0, 0))
        d_query = jnp.where(low, d_q[0], d_q[1]) * scale
        d_values = jnp.where(low, d_v[0], d_v[1])
        sacc[2:3, cols] += jnp.sum(d_query, axis=0, keepdims=True)
        sacc[3:4, cols] += jnp.sum(d_values, axis=0, keepdims=True)
        q_s[:, cols] = d_query.astype(bf16)
        k_s[:, cols] = jnp.where(low, d_k[0], d_k[1]).astype(bf16)
        v_s[:, cols] = d_values.astype(bf16)
    d_in = jnp.zeros_like(d_resid)
    for index, piece in enumerate((q_s, k_s, v_s)):
        d_mixed = piece[...]
        add(index, dot(attn_in, d_mixed, 0, 0))
        d_in = d_in + dot(d_mixed, weight(index), 1, 1)
    add_small(0, d_in * normed1)
    add_small(1, d_in)
    dimg_ref[0] = (d_resid + norm_back(d_in * vec(0), normed1, rstd1))[0:tokens, :]

    @pl.when(step == last)
    def _():
        big = acc.shape[1]
        g_ref[:, 0:big, :] = acc[...].astype(bf16)
        g_ref[:, big:, :] = jnp.broadcast_to(sacc[...][None], (BLOCKS, SMALL, width)).astype(bf16)


def repack(packed, count, small):
    if packed.shape[0] == count:
        return packed
    have, _, width = packed.shape
    pieces, start = [], 0
    total = packed.shape[1] - SMALL
    old = width // have
    ff_parts = (total - 4 * old) // (2 * old)
    for size in [old] * (4 + ff_parts) + [ff_parts * old]:
        piece = packed[:, start : start + size, :]
        pieces.append(piece.reshape(count, size * have // count, width))
        start += size
    pieces.append(small(packed[:, start:, :]))
    return jnp.concatenate(pieces, axis=1)


def gather_small(block):
    whole = jnp.sum(block.astype(jnp.float32), axis=0, keepdims=True).astype(block.dtype)
    return jnp.concatenate([whole, jnp.zeros((BLOCKS - 1,) + whole.shape[1:], block.dtype)], axis=0)


def run_blocks(alive, images, cotangent, packed):
    count, tokens, width = images.shape
    rows = -(-tokens // 16) * 16
    big = packed.shape[1] - SMALL
    one = lambda i: (i, 0, 0)
    fixed = lambda i: (0, 0, 0)
    return pl.pallas_call(
        functools.partial(block_kernel, count - 1, tokens),
        grid=(count,),
        in_specs=[
            pl.BlockSpec(memory_space=pltpu.SMEM),
            pl.BlockSpec((1, tokens, width), one),
            pl.BlockSpec((1, tokens, width), one),
            pl.BlockSpec(packed.shape, fixed),
        ],
        out_specs=[
            pl.BlockSpec((1, tokens, width), one),
            pl.BlockSpec((1, tokens, width), one),
            pl.BlockSpec(packed.shape, fixed),
        ],
        out_shape=[
            jax.ShapeDtypeStruct(images.shape, jnp.bfloat16),
            jax.ShapeDtypeStruct(images.shape, jnp.float32),
            jax.ShapeDtypeStruct(packed.shape, jnp.bfloat16),
        ],
        scratch_shapes=[
            pltpu.VMEM((rows, width), jnp.float32),
            pltpu.VMEM((rows, width), jnp.float32),
            pltpu.VMEM((BLOCKS, big, width), jnp.float32),
            pltpu.VMEM((SMALL, width), jnp.float32),
            pltpu.VMEM((H, rows, rows), jnp.float32),
            pltpu.VMEM((rows, width), jnp.bfloat16),
            pltpu.VMEM((rows, width), jnp.bfloat16),
            pltpu.VMEM((rows, width), jnp.bfloat16),
            pltpu.VMEM((rows, width), jnp.bfloat16),
        ],
        compiler_params=pltpu.CompilerParams(vmem_limit_bytes=62 * 1024 * 1024),
    )(alive, images, cotangent, packed)


def shards(
    images, cotangent, image_counts, ln1_gain, ln1_bias, qkv_weight, q_bias, v_bias,
    out_weight, out_bias, ln2_gain, ln2_bias, fc1_weight, fc1_bias, fc2_weight, fc2_bias,
):
    micro, slots, tokens, width = images.shape
    shards_count = lax.axis_size("fsdp")
    me = lax.axis_index("fsdp")
    own = ln1_gain.shape[0]
    hidden = fc1_bias.shape[0] * shards_count
    ff_parts = hidden // width
    alive = (jnp.arange(slots)[None, :] < image_counts).astype(jnp.float32).reshape(micro * slots)

    vectors = jnp.stack([ln1_gain, ln1_bias, q_bias, v_bias, out_bias, ln2_gain, ln2_bias, fc2_bias])
    narrow = lax.dynamic_update_slice(jnp.zeros((8, width), jnp.bfloat16), vectors, (0, me * own))
    wide = lax.dynamic_update_slice(jnp.zeros((hidden,), jnp.bfloat16), fc1_bias, (me * fc1_bias.shape[0],))
    wide = wide.reshape(ff_parts, width)
    spare = jnp.zeros((SMALL - 8 - ff_parts, width), jnp.bfloat16)
    cuts = [qkv_weight[:, i * width : (i + 1) * width] for i in range(3)]
    cuts.append(out_weight)
    cuts += [fc1_weight[:, i * width : (i + 1) * width] for i in range(ff_parts)]
    mine = jnp.concatenate(cuts + [fc2_weight, narrow, wide, spare], axis=0)

    gathered = lax.all_gather(mine, "fsdp", axis=0)
    packed = repack(gathered, BLOCKS, gather_small)
    block_out, image_grad, grads = run_blocks(
        alive,
        images.reshape(micro * slots, tokens, width),
        cotangent.reshape(micro * slots, tokens, width),
        packed,
    )
    grads = repack(
        grads,
        shards_count,
        lambda block: jnp.broadcast_to(block[:1], (shards_count,) + block.shape[1:]),
    )
    swapped = lax.all_to_all(grads, "fsdp", 0, 0)
    total = jnp.sum(swapped.astype(jnp.float32), axis=0).astype(jnp.bfloat16)
    copies = lax.all_gather(total, "dp", axis=0)
    total = jnp.sum(copies.astype(jnp.float32), axis=0)

    def cut(index):
        return total[index * own : (index + 1) * own]

    start = (4 + ff_parts) * own
    end = start + fc2_weight.shape[0]
    narrow = lax.dynamic_slice(total[end : end + 8], (0, me * own), (8, own))
    wide = lax.dynamic_slice(
        total[end + 8 : end + 8 + ff_parts].reshape(hidden), (me * fc1_bias.shape[0],), fc1_bias.shape
    )
    return (
        block_out.reshape(images.shape),
        image_grad.reshape(images.shape),
        narrow[0],
        narrow[1],
        jnp.concatenate([cut(i) for i in range(3)], axis=1),
        narrow[2],
        narrow[3],
        cut(3),
        narrow[4],
        narrow[5],
        narrow[6],
        jnp.concatenate([cut(4 + i) for i in range(ff_parts)], axis=1),
        wide,
        total[start:end],
        narrow[7],
    )


def solution(mesh):
    spread = P(None, ("dp", "fsdp"), None, None)
    row = P("fsdp", None)
    one = P("fsdp")
    return jax.shard_map(
        shards,
        mesh=mesh,
        in_specs=(
            spread, spread, P(None, ("dp", "fsdp")), one, one, row, one, one,
            row, one, one, one, row, one, row, one,
        ),
        out_specs=(
            spread, spread, one, one, row, one, one, row, one, one, one, row, one, row, one,
        ),
        check_vma=False,
    )
```

time: 350 us -> 202 us (0.58)
  matrix products: 58.3 us -> 0 us
  waiting for transfers between devices: 129 us -> 71.7 us
  Pallas kernels: 0 us -> 41.9 us
  blocking collectives: 88.3 us -> 47.5 us
  other arithmetic: 23.8 us -> 6.89 us
  local copies, waits for them, and re-layouts: 30.9 us -> 19.7 us
  between operations: 18 us -> 14.2 us
    reduce_scatter x4 -> x0, waiting for transfers between devices: 113 us -> none  [the longest x1 44 us: shards(): lax.psum_scatter(totals[9], 'fsdp', scatter_dimension=0, tiled=True)]
    all_gather x2, waiting for transfers between devices: 0.01 us -> 71.7 us  [the longest x1 37.4 us: shards(): copies = lax.all_gather(total, 'dp', axis=0)]
    dot_general x36 -> x0, matrix products: 58.3 us -> none  [product(): return jnp.einsum(form, left, right, preferred_element_type=jnp.float32)]
    unnamed x2 -> x0, blocking collectives: 48.6 us -> none
    all_to_all x0 -> x1, blocking collectives: none -> 47.5 us  [shards(): swapped = lax.all_to_all(grads, 'fsdp', 0, 0)]
    pallas_call x0 -> x1, Pallas kernels: none -> 41.9 us  [run_blocks(): pl.pallas_call(functools.partial(block_kernel, count - 1, tokens), grid=(...]
    all_gather x2 -> x0, blocking collectives: 19.9 us -> none  [the longest x1 11.2 us: shards(): lax.all_gather(qkv_weight, 'fsdp', axis=0, tiled=True)]
    psum x1 -> x0, blocking collectives: 19.8 us -> none  [shards(): lax.psum(totals[0].astype(jnp.bfloat16), 'dp').astype(jnp.float32)]
  transfers between devices with their start and end apart: 7 -> 2, of which waited for: 5 -> 2; matrix products, arithmetic and copies ran while one was open for 19% -> 3% of each run, Pallas kernels for 0% -> 0%
where the time goes in v1:
time: 202 us
  waiting for transfers between devices  71.7 us (35%)
  blocking collectives  47.5 us (24%)
  Pallas kernels  41.9 us (21%)
  local copies, waits for them, and re-layouts  19.7 us (10%)
  between operations  14.2 us (7%)
  other arithmetic  6.89 us (3%)
    all_to_all x1, blocking collectives, shards(): swapped = lax.all_to_all(grads, 'fsdp', 0, 0)  47.5 us
    pallas_call x1, Pallas kernels, run_blocks(): pl.pallas_call(functools.partial(block_kernel, count - 1, tokens), grid=(...  41.9 us
    all_gather x1, waiting for transfers between devices, shards(): copies = lax.all_gather(total, 'dp', axis=0)  37.4 us
    all_gather x1, waiting for transfers between devices, shards(): gathered = lax.all_gather(mine, 'fsdp', axis=0)  34.4 us
    concatenate x1, local copies, waits for them, and re-layouts, shards(): mine = jnp.concatenate(cuts + [fc2_weight, narrow, wide, spare], axis=0)  8.53 us
    unnamed x14, local copies, waits for them, and re-layouts  5.07 us
  transfers between devices with their start and end apart: 2, of which 2 were waited for; matrix products, arithmetic and copies ran while one was open for 3% of the time, Pallas kernels for 0%

profile of v1, /device:TPU:0, one launch (start us, length us, event | category | flops | bytes accessed | tf_op | source)
XLA Modules:
  0.0 202.1 jit_solution(15855715123842038974)
XLA Ops:
  7.3 1.0 dynamic_update_slice.7
  8.3 0.9 fusion.1
  9.2 0.8 stack.35
  10.0 0.2 dynamic_update_slice.6
  10.2 8.5 %concatenate.9 = bf16[592,384]{1,0:T(8,128)(2,1)} concatenate(bf16[48,384]{1,0:T(8,128)(2,1)S(1)} %get-tuple-element.75, bf16[48,384]{1,0:T(8,128)(2,1)S(1)} %get-tuple-element.74, bf16[48,384]{1,0:T(8,128)(2,1)S(1)} %get-tuple-element.76, bf16[48,384]{1,0:T(8,128)(2,1)} %param.24, bf16[48,384]{1,0:T(8,128)(2,1)S(1)} %get-tuple-element.61, ...), dimensions={0} | concatenate | bytes 909312 | tf_op jit(solution)/shard_map/concatenate | solution.py:259
  18.8 0.1 compare_convert_fusion
  18.8 0.6 reshape.60.alive_ref
  19.4 0.9 copy.35
  20.3 1.2 copy.36
  21.6 34.4 %all-gather.5.cloned.1.call-done = bf16[4736,384]{1,0:T(8,128)(2,1)} async-done(((bf16[592,384]{1,0:T(8,128)(2,1)}), bf16[4736,384]{1,0:T(8,128)(2,1)}) %all-gather.5.cloned.1.call-update) | async-done | bytes 3637264 | tf_op jit(solution)/shard_map/all_gather | solution.py:261
  55.9 41.9 %shard_map.271 = (bf16[4,197,384]{2,1,0:T(8,128)(2,1)}, f32[4,197,384]{2,1,0:T(8,128)}, bf16[8,592,384]{2,1,0:T(8,128)(2,1)}) custom-call(f32[4]{0:T(128)} %reshape.60.alive_ref, bf16[4,197,384]{2,1,0:T(8,128)(2,1)} %bitcast.34, f32[4,197,384]{2,1,0:T(8,128)} %bitcast.32, bf16[8,592,384]{2,1,0:T(8,128)(2,1)} %bitcast.33), custom_call_target="tpu_custom_call" | custom-call | tf_op jit(solution)/shard_map/pallas_call | solution.py:205
  97.8 47.5 %all_to_all.5 = bf16[8,592,384]{2,1,0:T(8,128)(2,1)} all-to-all(bf16[8,592,384]{2,1,0:T(8,128)(2,1)} %get-tuple-element.20), channel_id=1, replica_groups=mesh['dp'=4,'fsdp'=8] {'fsdp'}, dimensions={0} | all-to-all | bytes 7274496 | tf_op jit(solution)/shard_map/all_to_all | solution.py:274
  145.4 3.5 %reduce_sum.21 = bf16[592,384]{1,0:T(8,128)(2,1)} reduce(bf16[8,592,384]{2,1,0:T(8,128)(2,1)} %all_to_all.5, bf16[]{:T(256)} %constant.8.clone.1), dimensions={0}, to_apply=%region_0.0 | reduce | flops 1591296 | bytes 4091906 | tf_op jit(solution)/shard_map/reduce_sum | solution.py:275
  148.9 1.3 copy.37
  150.2 1.6 copy.38
  151.8 37.4 %all-gather.7.cloned.1.call-done = bf16[2368,384]{1,0:T(8,128)(2,1)} async-done(((bf16[592,384]{1,0:T(8,128)(2,1)}), bf16[2368,384]{1,0:T(8,128)(2,1)}) %all-gather.7.cloned.1.call-update) | async-done | bytes 1818640 | tf_op jit(solution)/shard_map/all_gather | solution.py:276
  189.2 1.9 convert_reduce_fusion
  191.1 0.7 slice.114
  191.8 0.7 fusion
  192.5 0.6 dynamic_slice.7
  193.2 0.1 constant_dynamic-slice_fusion
  193.2 0.5 slice_bitcast_fusion
  193.8 0.7 pad_maximum_fusion.1
  194.5 0.7 pad_maximum_fusion
  (21 shorter events, 0.2 us)
Async XLA Ops:
  7.2 11.6 %copy-start.4 = (s32[2,1]{0,1:T(1,128)S(1)}, s32[2,1]{0,1:T(1,128)}, u32[]{:S(2)}) copy-start(s32[2,1]{0,1:T(1,128)} %param.18) | copy-start | bytes 28
  7.2 12.3 %copy-start.3 = (bf16[2,2,197,384]{3,1,2,0:T(2,128)(2,1)S(1)}, bf16[2,2,197,384]{3,1,2,0:T(2,128)(2,1)}, u32[]{:S(2)}) copy-start(bf16[2,2,197,384]{3,1,2,0:T(2,128)(2,1)} %param.16) | copy-start | bytes 1815556
  7.2 13.1 %copy-start.1 = (f32[2,2,197,384]{3,1,2,0:T(2,128)S(1)}, f32[2,2,197,384]{3,1,2,0:T(2,128)}, u32[]{:S(2)}) copy-start(f32[2,2,197,384]{3,1,2,0:T(2,128)} %param.17) | copy-start | bytes 3631108
  7.2 48.7 %all-gather.5.cloned.1.call-start = ((), (), s32[]{:S(2)}) async-start(), calls=%async_computation.1 | async-start | bytes 4091904 | tf_op jit(solution)/shard_map/all_gather | solution.py:261
  18.7 170.5 %all-gather.7.cloned.1.call-start = ((), (), s32[]{:S(2)}) async-start(), calls=%async_computation.2 | async-start | bytes 2273280 | tf_op jit(solution)/shard_map/all_gather | solution.py:276
  145.4 3.5 %copy-start.2 = (bf16[4,197,384]{2,1,0:T(8,128)(2,1)S(1)}, bf16[4,197,384]{2,1,0:T(8,128)(2,1)}, u32[]{:S(2)}) copy-start(bf16[4,197,384]{2,1,0:T(8,128)(2,1)} %get-tuple-element.18) | copy-start | bytes 1815556
  148.9 1.3 copy-start
Sparse Core Ops, SparseCore 0:
  18.8 37.0 all-gather.4
  149.0 40.1 all-gather.6

commit v2 on v1

--- a/solution.py
+++ b/solution.py
@@ -11,7 +11,9 @@
 HD = 64
 LANE = 128
 BLOCKS = 8
-SMALL = 16
+SMALL = 64
+VECTORS = 16
+CHUNKS = 5
 
 
 def dot(left, right, left_dim, right_dim):
@@ -60,7 +62,8 @@
     hid[0:tokens, :] = img_ref[0].astype(f32)
     cot[0:tokens, :] = cot_ref[0] * alive
 
-    small = jnp.sum(w_ref[:, w_ref.shape[1] - SMALL :, :].astype(f32), axis=0)
+    tail = w_ref.shape[1] - SMALL
+    small = jnp.sum(w_ref[:, tail : tail + VECTORS, :].astype(f32), axis=0)
 
     def vec(index):
         return small[index : index + 1, :]
@@ -173,6 +176,215 @@
         big = acc.shape[1]
         g_ref[:, 0:big, :] = acc[...].astype(bf16)
         g_ref[:, big:, :] = jnp.broadcast_to(sacc[...][None], (BLOCKS, SMALL, width)).astype(bf16)
+
+
+MESH = pl.DeviceIdType.MESH
+
+
+def neighbours():
+    me = lax.axis_index("fsdp")
+    core = lax.rem(me, 2)
+    chip = me // 2
+    x = lax.rem(chip, 2)
+    y = chip // 2
+    chips = (chip, y * 2 + 1 - x, (1 - y) * 2 + x, (1 - y) * 2 + 1 - x)
+    return me, core, chips
+
+
+def greet(devices):
+    barrier = pltpu.get_barrier_semaphore()
+    for device in devices:
+        pl.semaphore_signal(barrier, inc=1, device_id=device, device_id_type=MESH)
+    pl.semaphore_wait(barrier, len(devices))
+
+
+def gather_kernel(qkv_ref, proj_ref, one_ref, two_ref, small_ref, out_ref, mine_ref, send_sem, recv_sem):
+    me, core, chips = neighbours()
+    own, width = proj_ref.shape
+    start = 0
+    for source in (qkv_ref, proj_ref, one_ref):
+        for index in range(source.shape[1] // width):
+            mine_ref[start : start + own, :] = source[:, index * width : (index + 1) * width]
+            start += own
+    mine_ref[start : start + two_ref.shape[0], :] = two_ref[...]
+    mine_ref[start + two_ref.shape[0] :, :] = small_ref[...]
+    half = mine_ref.shape[0] // 2
+    partner = {"fsdp": chips[0] * 2 + 1 - core}
+    across = {"fsdp": chips[1] * 2 + core}
+    along = {"fsdp": chips[2] * 2 + core}
+    greet((partner, across, along))
+    started = []
+
+    def slot(chip, side, part):
+        return out_ref.at[chips[chip] * 2 + side, pl.ds(part * half, half)]
+
+    def send(index, source, target, device):
+        copy = pltpu.make_async_remote_copy(
+            src_ref=source, dst_ref=target, send_sem=send_sem.at[index],
+            recv_sem=recv_sem.at[index], device_id=device, device_id_type=MESH,
+        )
+        copy.start()
+        started.append(copy)
+
+    def wait(index, target):
+        pltpu.make_async_remote_copy(
+            src_ref=target, dst_ref=target, send_sem=send_sem.at[index],
+            recv_sem=recv_sem.at[index], device_id=partner, device_id_type=MESH,
+        ).wait_recv()
+
+    def own(part):
+        return mine_ref.at[pl.ds(part * half, half)]
+
+    for step in range(2):
+        send(2 + step, own(step), slot(0, core, step), across)
+        send(5 - step, own(1 - step), slot(0, core, 1 - step), along)
+    for part in range(2):
+        send(part, own(part), slot(0, core, part), partner)
+    out_ref[me] = mine_ref[...]
+    wait(2, slot(1, core, 0))
+    send(6, slot(1, core, 0), slot(1, core, 0), along)
+    wait(5, slot(2, core, 1))
+    send(7, slot(2, core, 1), slot(2, core, 1), across)
+    send(8, slot(1, core, 0), slot(1, core, 0), partner)
+    send(11, slot(2, core, 1), slot(2, core, 1), partner)
+    wait(3, slot(1, core, 1))
+    send(9, slot(1, core, 1), slot(1, core, 1), partner)
+    wait(4, slot(2, core, 0))
+    send(10, slot(2, core, 0), slot(2, core, 0), partner)
+    wait(6, slot(3, core, 0))
+    send(12, slot(3, core, 0), slot(3, core, 0), partner)
+    wait(7, slot(3, core, 1))
+    send(13, slot(3, core, 1), slot(3, core, 1), partner)
+    for part in range(2):
+        wait(part, slot(0, 1 - core, part))
+        wait(8 + part, slot(1, 1 - core, part))
+        wait(10 + part, slot(2, 1 - core, part))
+        wait(12 + part, slot(3, 1 - core, part))
+    for copy in started:
+        copy.wait_send()
+
+
+def reduce_kernel(
+    groups, g_ref, out_ref, from_partner, summed, from_chips, total, from_groups, quarter_sum, final,
+    partner_send, partner_recv, chip_send, chip_recv, group_send, group_recv, back_send, back_recv,
+):
+    me, core, chips = neighbours()
+    group = lax.axis_index("dp")
+    rows = g_ref.shape[1]
+    chunk = rows // CHUNKS
+    piece = chunk // groups
+    partner = {"fsdp": chips[0] * 2 + 1 - core}
+    peers = [{"fsdp": chips[k] * 2 + core} for k in range(4)]
+    others = [lax.rem(group + step, groups) for step in range(1, groups)]
+    greet([partner] + peers[1:] + [{"dp": other} for other in others])
+    f32, bf16 = jnp.float32, jnp.bfloat16
+    started = []
+
+    def copy(source, target, sends, receives, device):
+        made = pltpu.make_async_remote_copy(
+            src_ref=source, dst_ref=target, send_sem=sends, recv_sem=receives,
+            device_id=device, device_id_type=MESH,
+        )
+        made.start()
+        started.append(made)
+
+    def wait(target, sends, receives):
+        pltpu.make_async_remote_copy(
+            src_ref=target, dst_ref=target, send_sem=sends, recv_sem=receives,
+            device_id=partner, device_id_type=MESH,
+        ).wait_recv()
+
+    def span(c):
+        return pl.ds(c * chunk, chunk)
+
+    def quarter(c, owner):
+        return pl.ds(pl.multiple_of(c * chunk + owner * piece, piece), piece)
+
+    order = (3, 1, 2, 0)
+    for c in range(CHUNKS):
+        for k in order:
+            copy(
+                g_ref.at[chips[k] * 2 + 1 - core, span(c)], from_partner.at[k, span(c)],
+                partner_send.at[c, k], partner_recv.at[c, k], partner,
+            )
+    for c in range(CHUNKS):
+        for k in order:
+            wait(from_partner.at[k, span(c)], partner_send.at[c, k], partner_recv.at[c, k])
+            both = g_ref[chips[k] * 2 + core, span(c)].astype(f32) + from_partner[k, span(c)].astype(f32)
+            summed[k, span(c)] = both.astype(bf16)
+            if k:
+                copy(
+                    summed.at[k, span(c)], from_chips.at[k - 1, span(c)],
+                    chip_send.at[c, k], chip_recv.at[c, k], peers[k],
+                )
+    for c in range(CHUNKS):
+        whole = summed[0, span(c)].astype(f32)
+        for k in (1, 2, 3):
+            wait(from_chips.at[k - 1, span(c)], chip_send.at[c, k], chip_recv.at[c, k])
+            whole = whole + from_chips[k - 1, span(c)].astype(f32)
+        total[span(c)] = whole.astype(bf16)
+        for step, other in enumerate(others):
+            copy(
+                total.at[quarter(c, other)], from_groups.at[c, step],
+                group_send.at[c, step], group_recv.at[c, step], {"dp": other},
+            )
+    for c in range(CHUNKS):
+        whole = total[quarter(c, group)].astype(f32)
+        for step in range(groups - 1):
+            wait(from_groups.at[c, step], group_send.at[c, step], group_recv.at[c, step])
+            whole = whole + from_groups[c, step].astype(f32)
+        quarter_sum[c] = whole.astype(bf16)
+        final[quarter(c, group)] = whole.astype(bf16)
+        for step, other in enumerate(others):
+            copy(
+                quarter_sum.at[c], final.at[quarter(c, group)],
+                back_send.at[c, step], back_recv.at[c, step], {"dp": other},
+            )
+    for c in range(CHUNKS):
+        for step in range(groups - 1):
+            source = lax.rem(group + groups - 1 - step, groups)
+            wait(final.at[quarter(c, source)], back_send.at[c, step], back_recv.at[c, step])
+    out_ref[...] = final[...].astype(f32)
+    for made in started:
+        made.wait_send()
+
+
+def gather_shards(qkv, proj, one, two, small):
+    width = proj.shape[1]
+    rows = (qkv.size + proj.size + one.size + two.size + small.size) // width
+    return pl.pallas_call(
+        gather_kernel,
+        out_shape=jax.ShapeDtypeStruct((BLOCKS, rows, width), jnp.bfloat16),
+        in_specs=[pl.BlockSpec(memory_space=pltpu.VMEM)] * 5,
+        out_specs=pl.BlockSpec(memory_space=pltpu.VMEM),
+        scratch_shapes=[pltpu.VMEM((rows, width), jnp.bfloat16), pltpu.SemaphoreType.DMA((14,)), pltpu.SemaphoreType.DMA((14,))],
+        compiler_params=pltpu.CompilerParams(collective_id=0, has_side_effects=True),
+    )(qkv, proj, one, two, small)
+
+
+def reduce_shards(grads, groups):
+    _, rows, width = grads.shape
+    bf16 = jnp.bfloat16
+    piece = rows // CHUNKS // groups
+    dma = pltpu.SemaphoreType.DMA
+    return pl.pallas_call(
+        functools.partial(reduce_kernel, groups),
+        out_shape=jax.ShapeDtypeStruct((rows, width), jnp.float32),
+        in_specs=[pl.BlockSpec(memory_space=pltpu.VMEM)],
+        out_specs=pl.BlockSpec(memory_space=pltpu.VMEM),
+        scratch_shapes=[
+            pltpu.VMEM((4, rows, width), bf16),
+            pltpu.VMEM((4, rows, width), bf16),
+            pltpu.VMEM((3, rows, width), bf16),
+            pltpu.VMEM((rows, width), bf16),
+            pltpu.VMEM((CHUNKS, groups - 1, piece, width), bf16),
+            pltpu.VMEM((CHUNKS, piece, width), bf16),
+            pltpu.VMEM((rows, width), bf16),
+        ]
+        + [dma((CHUNKS, 4))] * 4
+        + [dma((CHUNKS, groups - 1))] * 4,
+        compiler_params=pltpu.CompilerParams(collective_id=1, has_side_effects=True),
+    )(grads)
 
 
 def repack(packed, count, small):
@@ -253,28 +465,34 @@
     wide = lax.dynamic_update_slice(jnp.zeros((hidden,), jnp.bfloat16), fc1_bias, (me * fc1_bias.shape[0],))
     wide = wide.reshape(ff_parts, width)
     spare = jnp.zeros((SMALL - 8 - ff_parts, width), jnp.bfloat16)
-    cuts = [qkv_weight[:, i * width : (i + 1) * width] for i in range(3)]
-    cuts.append(out_weight)
-    cuts += [fc1_weight[:, i * width : (i + 1) * width] for i in range(ff_parts)]
-    mine = jnp.concatenate(cuts + [fc2_weight, narrow, wide, spare], axis=0)
-
-    gathered = lax.all_gather(mine, "fsdp", axis=0)
-    packed = repack(gathered, BLOCKS, gather_small)
+    small = jnp.concatenate([narrow, wide, spare], axis=0)
+    groups = lax.axis_size("dp")
+    direct = shards_count == BLOCKS
+    if direct:
+        packed = gather_shards(qkv_weight, out_weight, fc1_weight, fc2_weight, small)
+    else:
+        cuts = [qkv_weight[:, i * width : (i + 1) * width] for i in range(3)]
+        cuts.append(out_weight)
+        cuts += [fc1_weight[:, i * width : (i + 1) * width] for i in range(ff_parts)]
+        mine = jnp.concatenate(cuts + [fc2_weight, small], axis=0)
+        packed = repack(lax.all_gather(mine, "fsdp", axis=0), BLOCKS, gather_small)
     block_out, image_grad, grads = run_blocks(
         alive,
         images.reshape(micro * slots, tokens, width),
         cotangent.reshape(micro * slots, tokens, width),
         packed,
     )
-    grads = repack(
-        grads,
-        shards_count,
-        lambda block: jnp.broadcast_to(block[:1], (shards_count,) + block.shape[1:]),
-    )
-    swapped = lax.all_to_all(grads, "fsdp", 0, 0)
-    total = jnp.sum(swapped.astype(jnp.float32), axis=0).astype(jnp.bfloat16)
-    copies = lax.all_gather(total, "dp", axis=0)
-    total = jnp.sum(copies.astype(jnp.float32), axis=0)
+    if direct:
+        total = reduce_shards(grads, groups)
+    else:
+        grads = repack(
+            grads,
+            shards_count,
+            lambda block: jnp.broadcast_to(block[:1], (shards_count,) + block.shape[1:]),
+        )
+        swapped = lax.all_to_all(grads, "fsdp", 0, 0)
+        total = jnp.sum(swapped.astype(jnp.float32), axis=0).astype(jnp.bfloat16)
+        total = jnp.sum(lax.all_gather(total, "dp", axis=0).astype(jnp.float32), axis=0)
 
     def cut(index):
         return total[index * own : (index + 1) * own]

time: 202 us -> 134 us (0.66)
  Pallas kernels: 41.9 us -> 114 us
  waiting for transfers between devices: 71.7 us -> 0 us
  blocking collectives: 47.5 us -> 0 us
  between operations: 14.2 us -> 0.71 us
  other arithmetic: 6.89 us -> 2.93 us
  local copies, waits for them, and re-layouts: 19.7 us -> 16 us
    all_gather x2 -> x0, waiting for transfers between devices: 71.7 us -> none  [the longest x1 37.4 us: shards(): copies = lax.all_gather(total, 'dp', axis=0)]
    pallas_call x0 -> x2, Pallas kernels: none -> 71.7 us  [the longest x1 46.2 us: reduce_shards(): pl.pallas_call(functools.partial(reduce_kernel, groups), out_shape=jax.Sh...]
    all_to_all x1 -> x0, blocking collectives: 47.5 us -> none  [shards(): swapped = lax.all_to_all(grads, 'fsdp', 0, 0)]
    concatenate x1, local copies, waits for them, and re-layouts: 8.53 us -> 0.08 us  [shards(): small = jnp.concatenate([narrow, wide, spare], axis=0)]
    reduce_sum x2 -> x0, other arithmetic: 5.38 us -> none  [the longest x1 3.51 us: shards(): total = jnp.sum(swapped.astype(jnp.float32), axis=0).astype(jnp.bfloat16)]
    unnamed x14 -> x8, local copies, waits for them, and re-layouts: 5.07 us -> 7.31 us
  transfers between devices with their start and end apart: 2 -> 0, of which waited for: 2 -> 0; matrix products, arithmetic and copies ran while one was open for 3% -> 0% of each run, Pallas kernels for 0% -> 0%
where the time goes in v2:
time: 134 us; the launch traced here: 133 us
  Pallas kernels  114 us (85%)
  local copies, waits for them, and re-layouts  16 us (12%)
  other arithmetic  2.93 us (2%)
    pallas_call x1, Pallas kernels, reduce_shards(): pl.pallas_call(functools.partial(reduce_kernel, groups), out_shape=jax.Sh...  46.2 us
    pallas_call x1, Pallas kernels, run_blocks(): pl.pallas_call(functools.partial(block_kernel, count - 1, tokens), grid=(...  42.1 us
    pallas_call x1, Pallas kernels, gather_shards(): pl.pallas_call(gather_kernel, out_shape=jax.ShapeDtypeStruct((BLOCKS, row...  25.5 us
    unnamed x8, local copies, waits for them, and re-layouts  7.31 us

profile of v2, /device:TPU:0, one launch (start us, length us, event | category | flops | bytes accessed | tf_op | source)
XLA Modules:
  0.0 133.5 jit_solution(15165069346110091530)
XLA Ops:
  0.6 0.0 copy-start.1
  0.7 0.1 pad.9.clone
  0.7 0.8 compare_convert_fusion
  1.6 0.6 reshape.60.alive_ref
  2.1 0.8 stack.35
  2.9 0.9 dynamic_update_slice.7
  3.8 0.2 dynamic_update_slice.6
  4.0 0.7 maximum_maximum_fusion.small_ref
  4.7 2.0 %copy.31 = bf16[2,2,197,384]{3,2,1,0:T(8,128)(2,1)} copy(bf16[2,2,197,384]{3,1,2,0:T(2,128)(2,1)} %param.16) | data formatting | bytes 1210368 | tf_op args[0]
  6.7 1.2 copy.32
  7.9 25.5 %shard_map.271.w_ref = bf16[8,640,384]{2,1,0:T(8,128)(2,1)} custom-call(bf16[48,1152]{1,0:T(8,128)(2,1)} %qkv_ref.1, bf16[48,384]{1,0:T(8,128)(2,1)} %proj_ref.1, bf16[48,1536]{1,0:T(8,128)(2,1)} %one_ref.1, bf16[192,384]{1,0:T(8,128)(2,1)} %two_ref.1, bf16[64,384]{1,0:T(8,128)(2,1)} %maximum_maximum_fusion.small_ref), custom_call_target="tpu_custom_call" | custom-call | tf_op jit(solution)/shard_map/pallas_call | solution.py:355
  33.4 42.1 %shard_map.272 = (bf16[4,197,384]{2,1,0:T(8,128)(2,1)}, f32[4,197,384]{2,1,0:T(8,128)}, bf16[8,640,384]{2,1,0:T(8,128)(2,1)}) custom-call(f32[4]{0:T(128)} %reshape.60.alive_ref, bf16[4,197,384]{2,1,0:T(8,128)(2,1)} %bitcast.30, f32[4,197,384]{2,1,0:T(8,128)} %bitcast.29, bf16[8,640,384]{2,1,0:T(8,128)(2,1)} %shard_map.271.w_ref), custom_call_target="tpu_custom_call" | custom-call | tf_op jit(solution)/shard_map/pallas_call | solution.py:417
  75.5 2.5 %copy.33 = bf16[2,2,197,384]{3,1,2,0:T(2,128)(2,1)} copy(bf16[2,2,197,384]{3,2,1,0:T(8,128)(2,1)} %bitcast.32) | data formatting | bytes 1210368
  78.0 1.6 %copy.34 = f32[2,2,197,384]{3,1,2,0:T(2,128)} copy(f32[2,2,197,384]{3,2,1,0:T(8,128)S(1)} %bitcast.31) | data formatting | bytes 2420736
  79.6 46.2 %shard_map.273 = f32[640,384]{1,0:T(8,128)} custom-call(bf16[8,640,384]{2,1,0:T(8,128)(2,1)} %get-tuple-element.20.g_ref), custom_call_target="tpu_custom_call" | custom-call | tf_op jit(solution)/shard_map/pallas_call | solution.py:370
  125.8 0.7 slice.73
  126.6 0.6 dynamic_slice.7
  127.2 0.7 slice.57
  127.9 0.1 constant_dynamic-slice_fusion
  128.0 0.5 slice_bitcast_fusion
  128.5 1.7 %slice.74 = f32[192,384]{1,0:T(8,128)} slice(f32[640,384]{1,0:T(8,128)} %shard_map.273), slice={[384:576], [0:384]} | slice | bytes 589824 | tf_op jit(solution)/shard_map/slice | solution.py:520
  130.2 1.8 %fusion = (f32[48,384]{1,0:T(8,128)S(1)}, f32[48,384]{1,0:T(8,128)S(1)}, f32[48,384]{1,0:T(8,128)S(1)}, f32[48,384]{1,0:T(8,128)S(1)}, f32[48,384]{1,0:T(8,128)}...) fusion(f32[640,384]{1,0:T(8,128)} %shard_map.273), kind=kLoop, calls=%fused_computation.13 | loop fusion | bytes 1179648 | tf_op jit(solution)/shard_map/slice | solution.py:498
  132.0 0.7 pad_maximum_fusion
  132.8 0.7 pad_maximum_fusion.1
  (8 shorter events, 0.0 us)
Async XLA Ops:
  0.6 6.0 %copy-start.1 = (f32[2,2,197,384]{3,1,2,0:T(2,128)S(1)}, f32[2,2,197,384]{3,1,2,0:T(2,128)}, u32[]{:S(2)}) copy-start(f32[2,2,197,384]{3,1,2,0:T(2,128)} %param.17) | copy-start | bytes 3631108
  75.5 2.5 %copy-start = (f32[4,197,384]{2,1,0:T(8,128)S(1)}, f32[4,197,384]{2,1,0:T(8,128)}, u32[]{:S(2)}) copy-start(f32[4,197,384]{2,1,0:T(8,128)} %get-tuple-element.19) | copy-start | bytes 3631108
